TPU v7x, 512 devices: a whole 4x4x16 slice. The times are simulated.
512 devices in a mesh: dp: 16 (over y, x), expert: 32 (over z, core).
Axes of the slice: x: 4, y: 4, z: 16, core: 2. Of those that a mesh axis runs over, the one named last changes fastest.
Arguments:
- tokens: bfloat16 [65536, 1024], P(('dp', 'expert')), may hold values from -6 to 6
- cotangent: bfloat16 [65536, 1024], P(('dp', 'expert')), may hold values from -4 to 4
- expert_ids: int32 [65536, 8], P(('dp', 'expert')), may hold values from 0 to 31, all different within a row; in each aligned block of 128 rows (0 to 127, 128 to 255, ...) at most 36 rows name the same one
- gate_probs: bfloat16 [65536, 8], P(('dp', 'expert')), may hold values from 0.049804688 to 0.29882812
- w_gate: bfloat16 [32, 1024, 384], P('expert'), may hold values from -0.1875 to 0.1875
- w_up: bfloat16 [32, 1024, 384], P('expert'), may hold values from -0.1875 to 0.1875
- w_down: bfloat16 [32, 384, 1024], P('expert'), may hold values from -0.3125 to 0.3125
Outputs:
- grad_tokens: bfloat16 [65536, 1024], P(('dp', 'expert'))
- grad_probs: bfloat16 [65536, 8], P(('dp', 'expert'))
- grad_w_gate: bfloat16 [32, 1024, 384], P('expert', 'dp')
- grad_w_up: bfloat16 [32, 1024, 384], P('expert', 'dp')
- grad_w_down: bfloat16 [32, 384, 1024], P('expert', 'dp')
Inputs may be any that keep to these rules, and one draw needn't show every extreme that they name: `expert_ids`: each row names 8 different experts. Among the rows of one device no expert is named more than 36 times, and in some device's rows some expert is named exactly 36 times.
All inputs are finite; a program needn't handle non-finite values.
Results may differ from a plain program's by a relative error of at most 0.014.
Values may be sent and summed in bfloat16 or wider, within the bound.
A program may use at most 64 MiB of HBM per device.

v0:
```python
import jax
import jax.numpy as jnp
from jax import lax
from jax.sharding import PartitionSpec as P


def silu_parts(gate):
    sig = jax.nn.sigmoid(gate)
    return (gate * sig, sig + gate * sig * (1.0 - sig))


def on_device(tokens, cotangent, expert_ids, gate_probs, w_gate, w_up, w_down):
    tok_dev, width = tokens.shape
    topk = expert_ids.shape[1]
    local = w_gate.shape[0]
    experts = local * lax.axis_size("expert")
    most = min(tok_dev, tok_dev * topk * 9 // (8 * experts))
    assigns = tok_dev * topk
    flat_ids = expert_ids.reshape(assigns)
    onehot = (flat_ids[:, None] == jnp.arange(experts, dtype=jnp.int32)[None, :]).astype(jnp.int32)
    ranks = jnp.cumsum(onehot, axis=0) - 1
    slots = jnp.sum(ranks * onehot, axis=1)
    target = flat_ids * most + slots
    filled = (
        jnp.full((experts * most,), assigns, jnp.int32)
        .at[target]
        .set(jnp.arange(assigns, dtype=jnp.int32))
    )
    rows_tok = filled // topk
    zero_row = jnp.zeros((1, width), jnp.bfloat16)
    x_slots = jnp.concatenate([tokens, zero_row], axis=0)[rows_tok].reshape(experts, most, width)
    dy_slots = jnp.concatenate([cotangent, zero_row], axis=0)[rows_tok].reshape(
        experts, most, width
    )
    p_flat = jnp.concatenate([gate_probs.reshape(assigns), jnp.zeros((1,), jnp.bfloat16)], axis=0)
    p_slots = p_flat[filled].reshape(experts, most)
    x_recv = lax.all_to_all(x_slots, "expert", split_axis=0, concat_axis=1, tiled=True)
    dy_recv, p_recv = (
        lax.all_to_all(dy_slots, "expert", split_axis=0, concat_axis=1, tiled=True),
        lax.all_to_all(p_slots, "expert", split_axis=0, concat_axis=1, tiled=True),
    )
    prob = p_recv.astype(jnp.float32)[:, :, None]
    gate = jnp.einsum("erd,edf->erf", x_recv, w_gate, preferred_element_type=jnp.float32)
    up = jnp.einsum("erd,edf->erf", x_recv, w_up, preferred_element_type=jnp.float32)
    act, dact = silu_parts(gate)
    hidden = (act * up).astype(jnp.bfloat16)
    scaled = (prob * dy_recv.astype(jnp.float32)).astype(jnp.bfloat16)
    grad_down_part = jnp.einsum("erf,erd->efd", hidden, scaled, preferred_element_type=jnp.float32)
    dz = jnp.einsum("erd,efd->erf", dy_recv, w_down, preferred_element_type=jnp.float32)
    gate_grad = jnp.sum(dz * hidden.astype(jnp.float32), axis=2).astype(jnp.bfloat16)
    dh = prob * dz
    d_gate = (dh * up * dact).astype(jnp.bfloat16)
    d_up = (dh * act).astype(jnp.bfloat16)
    row_grad = (
        jnp.einsum("erf,edf->erd", d_gate, w_gate, preferred_element_type=jnp.float32)
        + jnp.einsum("erf,edf->erd", d_up, w_up, preferred_element_type=jnp.float32)
    ).astype(jnp.bfloat16)
    back_rows, back_probs = (
        lax.all_to_all(row_grad, "expert", split_axis=1, concat_axis=0, tiled=True),
        lax.all_to_all(gate_grad, "expert", split_axis=1, concat_axis=0, tiled=True),
    )
    grad_gate_part = jnp.einsum("erd,erf->edf", x_recv, d_gate, preferred_element_type=jnp.float32)
    grad_up_part = jnp.einsum("erd,erf->edf", x_recv, d_up, preferred_element_type=jnp.float32)
    summed_gate, summed_up, summed_down = (
        lax.psum_scatter(
            grad_gate_part.astype(jnp.bfloat16), "dp", scatter_dimension=1, tiled=True
        ).astype(jnp.float32),
        lax.psum_scatter(
            grad_up_part.astype(jnp.bfloat16), "dp", scatter_dimension=1, tiled=True
        ).astype(jnp.float32),
        lax.psum_scatter(
            grad_down_part.astype(jnp.bfloat16), "dp", scatter_dimension=1, tiled=True
        ).astype(jnp.float32),
    )
    picked = back_rows.reshape(experts * most, width)[target].reshape(tok_dev, topk, width)
    grad_tokens = jnp.sum(picked.astype(jnp.float32), axis=1).astype(jnp.bfloat16)
    grad_probs = back_probs.reshape(experts * most)[target].reshape(tok_dev, topk)
    return (
        grad_tokens,
        grad_probs,
        summed_gate.astype(jnp.bfloat16),
        summed_up.astype(jnp.bfloat16),
        summed_down.astype(jnp.bfloat16),
    )


def solution(mesh):
    return jax.shard_map(
        on_device,
        mesh=mesh,
        in_specs=(
            P(("dp", "expert"), None),
            P(("dp", "expert"), None),
            P(("dp", "expert"), None),
            P(("dp", "expert"), None),
            P("expert", None, None),
            P("expert", None, None),
            P("expert", None, None),
        ),
        out_specs=(
            P(("dp", "expert"), None),
            P(("dp", "expert"), None),
            P("expert", "dp", None),
            P("expert", "dp", None),
            P("expert", "dp", None),
        ),
        check_vma=False,
    )
```

profile of v0, /device:TPU:6, one launch (start us, length us, event | category | flops | bytes accessed | tf_op | source)
XLA Modules:
  0.0 664.8 jit_solution(12494220783853797060)
XLA Ops:
  10.0 9.0 %reduce-window.6 = s32[32,8,128]{2,1,0:T(8,128)S(1)} reduce-window(s32[32,8,128]{2,1,0:T(8,128)S(1)} %fusion.20, s32[]{:T(128)} %constant.17.clone.1), window={size=1x1x128 pad=0_0x0_0x127_0}, to_apply=%region_0.0 | reduce-window | flops 4161536 | bytes 262148 | tf_op jit(solution)/shard_map/reduce-window
  19.6 4.3 scatter_custom_fusion
  24.0 7.3 %gather_fusion = bf16[1152]{0:T(1024)(128)(2,1)S(1)} fusion(bf16[1025]{0:T(1024)(128)(2,1)S(1)} %pad_maximum_fusion, s32[2048]{0:T(1024)S(1)} %get-tuple-element.27), kind=kCustom, calls=%fused_computation | custom fusion | bytes 9216 | tf_op jit(solution)/shard_map/gather | solution.py:36
  32.0 15.5 %all-to-all-start = ((bf16[32,1,36]{2,1,0:T(2,128)(2,1)}), bf16[32,1,36]{2,1,0:T(2,128)(2,1)S(1)}, u32[]{:S(2)}, u32[]{:S(2)}) async-start(bf16[32,1,36]{2,1,0:T(2,128)(2,1)} %all_to_all.20), calls=%async_computation | async-start | bytes 32768 | tf_op jit(solution)/shard_map/all_to_all | solution.py:40
  47.5 4.4 gather_fusion.2
  51.9 2.2 reshape.230
  54.1 5.8 all-to-all-done
  59.9 6.6 all-to-all-start.2
  66.5 4.4 gather_fusion.1
  73.1 113.7 %all-to-all-done.2 = bf16[32,36,1024]{2,1,0:T(8,128)(2,1)} async-done(((bf16[32,36,1024]{2,1,0:T(8,128)(2,1)}), bf16[32,36,1024]{2,1,0:T(8,128)(2,1)}, u32[]{:S(2)}, u32[]{:S(2)}) %all-to-all-start.2) | async-done | bytes 2359328 | tf_op jit(solution)/shard_map/all_to_all | solution.py:37
  186.8 5.9 all-to-all-start.1
  192.8 4.1 reshape.231
  196.9 4.2 fusion.11
  201.2 2.5 fusion.14
  203.7 109.3 %all-to-all-done.1 = bf16[32,36,1024]{2,1,0:T(8,128)(2,1)S(1)} async-done(((bf16[32,36,1024]{2,1,0:T(8,128)(2,1)}), bf16[32,36,1024]{2,1,0:T(8,128)(2,1)S(1)}, u32[]{:S(2)}, u32[]{:S(2)}) %all-to-all-start.1) | async-done | bytes 2359328 | tf_op jit(solution)/shard_map/all_to_all | solution.py:39
  315.1 5.7 multiply_reduce_fusion
  321.6 6.0 all-to-all-start.4
  330.7 16.4 %copy.46 = bf16[1,1152,1024]{2,0,1:T(2,128)(2,1)} copy(bf16[1,1152,1024]{2,1,0:T(8,128)(2,1)S(1)} %fusion.1) | data formatting | bytes 4718592 | tf_op jit(solution)/shard_map/convert_element_type | solution.py:57
  347.6 14.2 %reduce.8 = bf16[1152,1024]{1,0:T(8,128)(2,1)S(1)} reduce(bf16[1152,1,1024]{2,1,0:T(2,128)(2,1)} %bitcast.63, bf16[]{:T(256)} %broadcast.132), dimensions={1}, to_apply=%bitcast.60.reduce_sub_computation | reduce | bytes 4718594
  361.8 2.8 reshape.303
  364.6 12.0 %all-to-all-start.3 = ((bf16[32,2,18432]{2,1,0:T(2,128)(2,1)}), bf16[32,2,18432]{2,1,0:T(2,128)(2,1)S(1)}, u32[]{:S(2)}, u32[]{:S(2)}) async-start(bf16[32,2,18432]{2,1,0:T(2,128)(2,1)} %reshape.303), calls=%async_computation.3 | async-start | bytes 4718592 | tf_op jit(solution)/shard_map/all_to_all | solution.py:59
  376.6 4.1 fusion.7
  380.9 4.3 fusion.6
  385.4 4.3 fusion.5
  389.9 6.8 %gather_fusion.4 = bf16[1024]{0:T(1024)(128)(2,1)S(1)} fusion(bf16[1152]{0:T(1024)(128)(2,1)S(1)} %reshape.236, s32[1024]{0:T(1024)S(1)} %broadcast_clamp_fusion), kind=kCustom, calls=%fused_computation.4 | custom fusion | bytes 8192 | tf_op jit(solution)/shard_map/gather | solution.py:77
  397.5 88.8 %all-to-all-done.3 = bf16[32,2,18432]{2,1,0:T(2,128)(2,1)S(1)} async-done(((bf16[32,2,18432]{2,1,0:T(2,128)(2,1)}), bf16[32,2,18432]{2,1,0:T(2,128)(2,1)S(1)}, u32[]{:S(2)}, u32[]{:S(2)}) %all-to-all-start.3) | async-done | bytes 2359328 | tf_op jit(solution)/shard_map/all_to_all | solution.py:59
  486.3 7.0 %reshape.304 = bf16[1152,1,1024]{2,1,0:T(2,128)(2,1)} reshape(bf16[32,2,18432]{2,1,0:T(2,128)(2,1)S(1)} %all-to-all-done.3) | data formatting | bytes 4718592
  493.2 3.3 copy.45
  496.5 5.4 gather_fusion.3
  501.9 3.7 bitcast_reduce_fusion
  505.6 59.5 %reduce-scatter.9.cloned.1.call-done = bf16[1,64,384]{2,1,0:T(8,128)(2,1)} async-done(((bf16[1,1024,384]{2,1,0:T(8,128)(2,1)}), bf16[1,64,384]{2,1,0:T(8,128)(2,1)}) %reduce-scatter.9.cloned.1.call-update) | async-done | bytes 49168 | tf_op jit(solution)/shard_map/reduce_scatter | solution.py:68
  565.1 93.2 %reduce-scatter.7.cloned.1.call-done = bf16[1,64,384]{2,1,0:T(8,128)(2,1)} async-done(((bf16[1,1024,384]{2,1,0:T(8,128)(2,1)}), bf16[1,64,384]{2,1,0:T(8,128)(2,1)}) %reduce-scatter.7.cloned.1.call-update) | async-done | bytes 49168 | tf_op jit(solution)/shard_map/reduce_scatter | solution.py:65
  (61 shorter events, 14.2 us)
Async XLA Ops:
  7.2 189.7 %copy-start = (bf16[1,1024,384]{2,1,0:T(8,128)(2,1)S(1)}, bf16[1,1024,384]{2,1,0:T(8,128)(2,1)}, u32[]{:S(2)}) copy-start(bf16[1,1024,384]{2,1,0:T(8,128)(2,1)} %param.11) | copy-start | bytes 2359300
  19.4 28.1 %copy-start.6 = (bf16[128,1024]{1,0:T(8,128)(2,1)S(1)}, bf16[128,1024]{1,0:T(8,128)(2,1)}, u32[]{:S(2)}) copy-start(bf16[128,1024]{1,0:T(8,128)(2,1)} %param.7) | copy-start | bytes 786436
  32.0 27.9 %all-to-all-start = ((bf16[32,1,36]{2,1,0:T(2,128)(2,1)}), bf16[32,1,36]{2,1,0:T(2,128)(2,1)S(1)}, u32[]{:S(2)}, u32[]{:S(2)}) async-start(bf16[32,1,36]{2,1,0:T(2,128)(2,1)} %all_to_all.20), calls=%async_computation | async-start | bytes 32768 | tf_op jit(solution)/shard_map/all_to_all | solution.py:40
  54.1 12.4 %copy-start.7 = (bf16[128,1024]{1,0:T(8,128)(2,1)S(1)}, bf16[128,1024]{1,0:T(8,128)(2,1)}, u32[]{:S(2)}) copy-start(bf16[128,1024]{1,0:T(8,128)(2,1)} %param.8) | copy-start | bytes 786436
  59.9 126.9 %all-to-all-start.2 = ((bf16[32,36,1024]{2,1,0:T(8,128)(2,1)}), bf16[32,36,1024]{2,1,0:T(8,128)(2,1)}, u32[]{:S(2)}, u32[]{:S(2)}) async-start(bf16[32,36,1024]{2,1,0:T(8,128)(2,1)} %reshape.230), calls=%async_computation.2 | async-start | bytes 5242880 | tf_op jit(solution)/shard_map/all_to_all | solution.py:37
  186.8 126.2 %all-to-all-start.1 = ((bf16[32,36,1024]{2,1,0:T(8,128)(2,1)}), bf16[32,36,1024]{2,1,0:T(8,128)(2,1)S(1)}, u32[]{:S(2)}, u32[]{:S(2)}) async-start(bf16[32,36,1024]{2,1,0:T(8,128)(2,1)} %reshape.227), calls=%async_computation.1 | async-start | bytes 5242880 | tf_op jit(solution)/shard_map/all_to_all | solution.py:39
  196.9 4.3 copy-start.1
  196.9 4.3 copy-start.4
  320.8 8.4 %copy-start.2 = (bf16[1152,384]{0,1:T(8,128)(2,1)}, bf16[1152,384]{0,1:T(8,128)(2,1)S(1)}, u32[]{:S(2)}) copy-start(bf16[1152,384]{0,1:T(8,128)(2,1)S(1)} %get-tuple-element.22) | copy-start | bytes 2654212
  320.8 8.4 %copy-start.3 = (bf16[1152,384]{0,1:T(8,128)(2,1)}, bf16[1152,384]{0,1:T(8,128)(2,1)S(1)}, u32[]{:S(2)}) copy-start(bf16[1152,384]{0,1:T(8,128)(2,1)S(1)} %get-tuple-element.23) | copy-start | bytes 2654212
  321.6 42.9 %all-to-all-start.4 = ((bf16[1,32,36]{2,0,1:T(2,128)(2,1)}), bf16[1,32,36]{2,0,1:T(2,128)(2,1)S(1)}, u32[]{:S(2)}, u32[]{:S(2)}) async-start(bf16[1,32,36]{2,0,1:T(2,128)(2,1)} %convert_element_type.120), calls=%async_computation.4 | async-start | bytes 32768 | tf_op jit(solution)/shard_map/all_to_all | solution.py:60
  327.7 1.5 copy-start.5
  364.6 121.7 %all-to-all-start.3 = ((bf16[32,2,18432]{2,1,0:T(2,128)(2,1)}), bf16[32,2,18432]{2,1,0:T(2,128)(2,1)S(1)}, u32[]{:S(2)}, u32[]{:S(2)}) async-start(bf16[32,2,18432]{2,1,0:T(2,128)(2,1)} %reshape.303), calls=%async_computation.3 | async-start | bytes 4718592 | tf_op jit(solution)/shard_map/all_to_all | solution.py:59
  376.6 129.0 %reduce-scatter.11.cloned.1.call-start = ((), (), s32[]{:S(2)}) async-start(), calls=%async_computation.10 | async-start | bytes 835584
  380.8 184.3 %reduce-scatter.9.cloned.1.call-start = ((), (), s32[]{:S(2)}) async-start(), calls=%async_computation.9 | async-start | bytes 835584 | tf_op jit(solution)/shard_map/reduce_scatter | solution.py:68
  385.2 273.1 %reduce-scatter.7.cloned.1.call-start = ((), (), s32[]{:S(2)}) async-start(), calls=%async_computation.8 | async-start | bytes 835584 | tf_op jit(solution)/shard_map/reduce_scatter | solution.py:65
Sparse Core Ops, SparseCore 0:
  382.0 89.8 reduce-scatter.10
  476.5 88.4 reduce-scatter.8
  569.7 88.4 reduce-scatter.6
where the time goes:
time: 666 us; the launch traced here: 665 us
  waiting for transfers between devices  470 us (71%)
  local copies, waits for them, and re-layouts  78 us (12%)
  starting transfers between devices  46.4 us (7%)
  matrix products  28.1 us (4%)
  other arithmetic  28 us (4%)
  between operations  14 us (2%)
    all_to_all x1, waiting for transfers between devices, on_device(): lax.all_to_all(x_slots, 'expert', split_axis=0, concat_axis=1, tiled=True)  114 us
    all_to_all x1, waiting for transfers between devices, on_device(): lax.all_to_all(dy_slots, 'expert', split_axis=0, concat_axis=1, tiled=True)  109 us
    reduce_scatter x1, waiting for transfers between devices, on_device(): lax.psum_scatter(grad_gate_part.astype(jnp.bfloat16), 'dp', scatter_dimen...  93.2 us
    all_to_all x1, waiting for transfers between devices, on_device(): lax.all_to_all(row_grad, 'expert', split_axis=1, concat_axis=0, tiled=True)  88.8 us
    reduce_scatter x1, waiting for transfers between devices, on_device(): lax.psum_scatter(grad_up_part.astype(jnp.bfloat16), 'dp', scatter_dimensi...  59.5 us
    convert_element_type x1, local copies, waits for them, and re-layouts, on_device(): row_grad = (jnp.einsum('erf,edf->erd', d_gate, w_gate, preferred_element_...  16.4 us
    unnamed x23, local copies, waits for them, and re-layouts  15.8 us
    all_to_all x1, starting transfers between devices, on_device(): lax.all_to_all(p_slots, 'expert', split_axis=0, concat_axis=1, tiled=True)  15.5 us
  transfers between devices with their start and end apart: 8, of which 6 were waited for; matrix products, arithmetic and copies ran while one was open for 15% of the time, Pallas kernels for 0%

commit v1 on v0

v1 whole, which is shorter than its diff:
```python
import functools

import jax
import jax.numpy as jnp
from jax import lax
from jax.experimental import pallas as pl
from jax.experimental.pallas import tpu as pltpu
from jax.sharding import PartitionSpec as P

MESH = pl.DeviceIdType.MESH
F32 = jnp.float32
BF16 = jnp.bfloat16
LANES = 128
STEP = 256


def contract(a, b, on_a, on_b):
    return lax.dot_general(a, b, (((on_a,), (on_b,)), ((), ())), preferred_element_type=F32)


def kernel(
    ids_ref, probs_ref, x_ref, dy_ref, wg_ref, wu_ref, wd_ref,
    gt_ref, gp_ref, og_ref, ou_ref, od_ref,
    x_all, dy_all, p_all, rows, grows, rpart, gpart, land, gland,
    wgu, wd, acc_gu, acc_d, gu, dz, dgu, hp,
    stage_g, stage_d, land_g, land_d,
    ag_s, ag_r, pc_s, pc_r, rp_s, rp_r, rs_s, rs_r, g_s, g_r, w_s, w_r, loc,
):
    ndp, nex = lax.axis_size("dp"), lax.axis_size("expert")
    me_dp, me = lax.axis_index("dp"), lax.axis_index("expert")
    steps = nex // 4
    tok, width = gt_ref.shape
    half = tok // 2
    ff = wd.shape[0]
    experts = p_all.shape[1]
    topk = ids_ref.shape[1]
    cut_g, cut_d = width // ndp, ff // ndp
    right = (me_dp, lax.rem(me + 2, nex))
    left = (me_dp, lax.rem(me + nex - 2, nex))
    partner = (me_dp, me + 1 - 2 * lax.rem(me, 2))
    toward = (right, left)
    peers = [(lax.rem(me_dp + j, ndp), me) for j in range(1, ndp)]

    def send(src, dst, ssem, rsem, dev):
        return pltpu.make_async_remote_copy(
            src_ref=src, dst_ref=dst, send_sem=ssem, recv_sem=rsem, device_id=dev, device_id_type=MESH
        )

    barrier = pltpu.get_barrier_semaphore()
    for dev in [right, left, partner] + peers:
        pl.semaphore_signal(barrier, inc=1, device_id=dev, device_id_type=MESH)
    local = [
        pltpu.make_async_copy(x_ref, x_all.at[0], loc.at[0]),
        pltpu.make_async_copy(dy_ref, dy_all.at[0], loc.at[1]),
        pltpu.make_async_copy(wg_ref.at[0], wgu.at[:, pl.ds(0, ff)], loc.at[2]),
        pltpu.make_async_copy(wu_ref.at[0], wgu.at[:, pl.ds(ff, ff)], loc.at[3]),
        pltpu.make_async_copy(wd_ref.at[0], wd, loc.at[4]),
    ]
    for copy in local:
        copy.start()
    pl.semaphore_wait(barrier, 3 + len(peers))

    streams = (x_all, dy_all)

    def own_slot(s, way):
        return 4 * s - 2 + way

    for k, src in ((0, x_ref), (1, dy_ref)):
        for way in range(2):
            send(src, streams[k].at[own_slot(1, way)], ag_s.at[k, 1, way], ag_r.at[k, 1, way], toward[way]).start()
        send(src, streams[k].at[1], pc_s.at[k, 0, 0], pc_r.at[k, 0, 0], partner).start()

    lane = lax.broadcasted_iota(jnp.int32, (tok, LANES), 1)
    table = jnp.zeros((tok, LANES), F32)
    for k in range(topk):
        table = jnp.where(lane == ids_ref[:, k : k + 1], probs_ref[:, k : k + 1].astype(F32), table)
    p_all[0] = table.T[:experts].astype(BF16)
    acc_gu[...] = jnp.zeros_like(acc_gu)
    acc_d[...] = jnp.zeros_like(acc_d)
    for way in range(2):
        send(p_all.at[0], p_all.at[own_slot(1, way)], ag_s.at[2, 1, way], ag_r.at[2, 1, way], toward[way]).start()
    send(p_all.at[0], p_all.at[1], pc_s.at[2, 0, 0], pc_r.at[2, 0, 0], partner).start()
    for copy in local:
        copy.wait()

    def part(way):
        return pl.ds(way * half, half)

    def full_in(k, ref, s, way):
        at = ref.at[own_slot(s, way)]
        return send(at, at, ag_s.at[k, s, way], ag_r.at[k, s, way], toward[way])

    def cross(k, ref, s, way):
        return send(
            ref.at[own_slot(s, way)], ref.at[4 * s + way], pc_s.at[k, s, way], pc_r.at[k, s, way], partner
        )

    def forward(k, ref, s, way):
        return send(
            ref.at[own_slot(s, way)], ref.at[own_slot(s + 1, way)],
            ag_s.at[k, s + 1, way], ag_r.at[k, s + 1, way], toward[way],
        )

    last_own, last_cross = 4 * steps - 2, 4 * steps - 1

    def forward_half(k, ref, way):
        return send(
            ref.at[own_slot(steps - 1, way), part(way)], ref.at[last_own, part(way)],
            ag_s.at[k, steps, way], ag_r.at[k, steps, way], toward[way],
        )

    def cross_half(k, ref, way):
        return send(
            ref.at[last_own, part(way)], ref.at[last_cross, part(way)],
            pc_s.at[k, steps, way], pc_r.at[k, steps, way], partner,
        )

    def forward_p_last():
        return send(
            p_all.at[own_slot(steps - 1, 0)], p_all.at[last_own],
            ag_s.at[2, steps, 0], ag_r.at[2, steps, 0], right,
        )

    def cross_p_last():
        return send(
            p_all.at[last_own], p_all.at[last_cross], pc_s.at[2, steps, 0], pc_r.at[2, steps, 0], partner
        )

    def poll(k, s):
        ref = streams[k]

        @pl.when(s < steps)
        def _():
            for way in range(2):
                full_in(k, ref, s, way).wait_recv()

                @pl.when(s < steps - 1)
                def _():
                    forward(k, ref, s, way).start()

                @pl.when(s == steps - 1)
                def _():
                    forward_half(k, ref, way).start()

                cross(k, ref, s, way).start()
            if k == 1:
                for way in range(2):
                    full_in(2, p_all, s, way).wait_recv()

                    @pl.when(s < steps - 1)
                    def _():
                        forward(2, p_all, s, way).start()

                    cross(2, p_all, s, way).start()

                @pl.when(s == steps - 1)
                def _():
                    forward_p_last().start()

        @pl.when(s == steps)
        def _():
            for way in range(2):
                forward_half(k, ref, way).wait_recv()
                cross_half(k, ref, way).start()
            if k == 1:
                forward_p_last().wait_recv()
                cross_p_last().start()

    def rows_out(i):
        return (
            send(rows.at[pl.ds(4 * i, 2)], rpart.at[pl.ds(2 * i - 1, 2)], rp_s.at[0, i], rp_r.at[0, i], partner),
            send(grows.at[pl.ds(4 * i, 2)], gpart.at[pl.ds(2 * i - 1, 2)], rp_s.at[1, i], rp_r.at[1, i], partner),
        )

    def rows_first():
        return (
            send(rows.at[1], rpart.at[0], rp_s.at[0, 0], rp_r.at[0, 0], partner),
            send(grows.at[1], gpart.at[0], rp_s.at[1, 0], rp_r.at[1, 0], partner),
        )

    def rows_last():
        return (
            send(rows.at[last_cross], rpart.at[2 * steps - 1], rp_s.at[0, steps], rp_r.at[0, steps], partner),
            send(grows.at[last_cross], gpart.at[2 * steps - 1], rp_s.at[1, steps], rp_r.at[1, steps], partner),
        )

    wide = 2 * tok
    pick = (lax.broadcasted_iota(jnp.int32, (experts, LANES), 0) == me).astype(F32).astype(BF16)

    def compute(u):
        at = pl.ds(2 * u, 2)
        for n in range(2 * ff // STEP):
            cols = pl.ds(n * STEP, STEP)
            gu[:, cols] = jnp.dot(
                x_all[at].reshape(wide, width), wgu[:, cols], preferred_element_type=F32
            )
        dz[...] = contract(dy_all[at].reshape(wide, width), wd[...], 1, 1)
        for b in range(2):
            prob = contract(p_all[2 * u + b], pick, 0, 0)
            gcol = []
            for r in range(0, tok, 32):
                chunk = pl.ds(b * tok + r, 32)
                pr = jnp.concatenate([prob[r : r + 32]] * (ff // LANES), axis=1)
                gate, up, back = gu[chunk, :ff], gu[chunk, ff:], dz[chunk, :]
                sig = jax.nn.sigmoid(gate)
                act = gate * sig
                hid = act * up
                gcol.append(jnp.sum(back * hid.astype(BF16).astype(F32), axis=1, keepdims=True))
                dh = pr * back
                dgu[chunk, :ff] = (dh * up * (sig + act * (1.0 - sig))).astype(BF16)
                dgu[chunk, ff:] = (dh * act).astype(BF16)
                hp[chunk, :] = (pr * hid).astype(BF16)
            column = jnp.concatenate(gcol, axis=0)
            grows[2 * u + b] = jnp.where(lane == me, column, 0.0).T[:experts].astype(BF16)
        for n in range(width // STEP):
            cols = pl.ds(n * STEP, STEP)
            rows[at, :, cols] = contract(dgu[...], wgu[cols, :], 1, 1).astype(BF16).reshape(2, tok, STEP)
        for n in range(width // STEP):
            cols = pl.ds(n * STEP, STEP)
            acc_gu[cols, :] += contract(x_all[at, :, cols].reshape(wide, STEP), dgu[...], 0, 0)
        for n in range(width // STEP):
            cols = pl.ds(n * STEP, STEP)
            acc_d[:, cols] += contract(hp[...], dy_all[at, :, cols].reshape(wide, STEP), 0, 0)

    def rs_copy(d, way, chunk, slot):
        return send(
            rows.at[slot, part(chunk)], land.at[way, d - 1, part(chunk)],
            rs_s.at[way, chunk, d - 1], rs_r.at[way, chunk, d - 1], toward[way],
        )

    def g_copy(d, way, slot):
        return send(
            grows.at[slot], gland.at[way, d - 1], g_s.at[way, d - 1], g_r.at[way, d - 1], toward[way]
        )

    def rs_flow(d, way, chunk, slot, other, first):
        lines = part(chunk)
        if not first:
            rs_copy(d + 1, way, chunk, slot).wait_recv()
        for r in range(0, half, 16):
            some = pl.ds(chunk * half + r, 16)
            total = rows[slot, some].astype(F32) + rpart[other, some].astype(F32)
            if not first:
                total = total + land[way, d, some].astype(F32)
            rows[slot, some] = total.astype(BF16)
        rs_copy(d, way, chunk, slot).start()
        if chunk == 0:
            if not first:
                g_copy(d + 1, way, slot).wait_recv()
            gsum = grows[slot].astype(F32) + gpart[other].astype(F32)
            if not first:
                gsum = gsum + gland[way, d].astype(F32)
            grows[slot] = gsum.astype(BF16)
            g_copy(d, way, slot).start()

    def near(d, way):
        return own_slot(d, 1 - way), 2 * d - way

    def unit(u, carry):
        i = u // 2
        even = lax.rem(u, 2) == 0

        @pl.when(u == 1)
        def _():
            poll(0, 1)

        @pl.when(jnp.logical_and(even, u > 0))
        def _():
            poll(0, i + 1)

        @pl.when(jnp.logical_not(even))
        def _():
            poll(1, i + 1)

        @pl.when(u == 0)
        def _():
            for k, ref in ((0, x_all), (1, dy_all), (2, p_all)):
                send(ref.at[0], ref.at[1], pc_s.at[k, 0, 0], pc_r.at[k, 0, 0], partner).wait_recv()

        @pl.when(jnp.logical_and(even, u > 0))
        def _():
            for k, ref in ((0, x_all), (1, dy_all), (2, p_all)):
                for way in range(2):
                    cross(k, ref, i, way).wait_recv()

        @pl.when(u == 2 * steps - 1)
        def _():
            for copy in rows_out(steps - 1):
                copy.wait_recv()
            for way in range(2):
                slot, other = near(steps - 1, way)
                rs_flow(steps - 1, way, 1 - way, slot, other, True)
            for way in range(2):
                cross_half(0, x_all, way).wait_recv()
                cross_half(1, dy_all, way).wait_recv()
            cross_p_last().wait_recv()

        compute(u)

        @pl.when(u == 0)
        def _():
            for copy in rows_first():
                copy.start()

        @pl.when(jnp.logical_and(even, u > 0))
        def _():
            for copy in rows_out(i):
                copy.start()

        @pl.when(u == 2 * steps - 1)
        def _():
            for copy in rows_last():
                copy.start()

        return carry

    lax.fori_loop(0, 2 * steps, unit, 0)

    for copy in rows_last():
        copy.wait_recv()
    for way in range(2):
        rs_flow(steps, way, way, last_own, 2 * steps - 1, True)

    def w_copies(j):
        to = lax.rem(me_dp + j, ndp)
        return (
            send(stage_g.at[to], land_g.at[j], w_s.at[0, j], w_r.at[0, j], (to, me)),
            send(stage_d.at[to], land_d.at[j], w_s.at[1, j], w_r.at[1, j], (to, me)),
        )

    for n in range(ndp):
        stage_g[n] = acc_gu[n * cut_g : (n + 1) * cut_g, :].astype(BF16)
    for n in range(ndp):
        stage_d[n] = acc_d[n * cut_d : (n + 1) * cut_d, :].astype(BF16)
    for j in range(1, ndp):
        for copy in w_copies(j):
            copy.start()

    def ring(t, carry):
        d = steps - 1 - t
        for way in range(2):
            slot, other = near(d, way)
            rs_flow(d, way, way, slot, other, False)

        @pl.when(d >= 2)
        def _():
            rp_wait = rows_out(d - 1)
            for copy in rp_wait:
                copy.wait_recv()
            for way in range(2):
                slot, other = near(d - 1, way)
                rs_flow(d - 1, way, 1 - way, slot, other, False)

        return carry

    lax.fori_loop(0, steps - 1, ring, 0)

    for copy in rows_first():
        copy.wait_recv()
    for way in range(2):
        rs_copy(1, way, 1 - way, 0).wait_recv()
    for way in range(2):
        rs_copy(1, way, way, 0).wait_recv()
        g_copy(1, way, 0).wait_recv()
    for r in range(0, tok, 16):
        some = pl.ds(r, 16)
        total = rows[0, some].astype(F32) + rpart[0, some].astype(F32)
        total = total + land[0, 0, some].astype(F32) + land[1, 0, some].astype(F32)
        gt_ref[some, :] = total.astype(BF16)
    gsum = grows[0].astype(F32) + gpart[0].astype(F32) + gland[0, 0].astype(F32) + gland[1, 0].astype(F32)
    if experts < LANES:
        gsum = jnp.concatenate([gsum, jnp.zeros((LANES - experts, tok), F32)], axis=0)
    gtab = gsum.T
    picked = []
    for k in range(topk):
        picked.append(
            jnp.sum(jnp.where(lane == ids_ref[:, k : k + 1], gtab, 0.0), axis=1, keepdims=True)
        )
    gp_ref[...] = jnp.concatenate(picked, axis=1).astype(BF16)

    for j in range(1, ndp):
        for copy in w_copies(j):
            copy.wait_recv()
    sum_g = stage_g[me_dp].astype(F32)
    sum_d = stage_d[me_dp].astype(F32)
    for j in range(1, ndp):
        sum_g = sum_g + land_g[j].astype(F32)
        sum_d = sum_d + land_d[j].astype(F32)
    og_ref[0] = sum_g[:, :ff].astype(BF16)
    ou_ref[0] = sum_g[:, ff:].astype(BF16)
    od_ref[0] = sum_d.astype(BF16)

    for k, src in ((0, x_ref), (1, dy_ref), (2, p_all.at[0])):
        ref = (x_all, dy_all, p_all)[k]
        for way in range(2):
            send(src, ref.at[own_slot(1, way)], ag_s.at[k, 1, way], ag_r.at[k, 1, way], toward[way]).wait_send()
        send(src, ref.at[1], pc_s.at[k, 0, 0], pc_r.at[k, 0, 0], partner).wait_send()

    def drain(s, carry):
        for k, ref in ((0, x_all), (1, dy_all), (2, p_all)):
            for way in range(2):
                cross(k, ref, s, way).wait_send()

                @pl.when(s < steps - 1)
                def _():
                    forward(k, ref, s, way).wait_send()

        for copy in rows_out(s):
            copy.wait_send()
        for way in range(2):
            slot, _ = near(s, way)
            for chunk in range(2):
                rs_copy(s, way, chunk, slot).wait_send()
            g_copy(s, way, slot).wait_send()
        return carry

    lax.fori_loop(1, steps, drain, 0)
    for k, ref in ((0, x_all), (1, dy_all)):
        for way in range(2):
            forward_half(k, ref, way).wait_send()
            cross_half(k, ref, way).wait_send()
    forward_p_last().wait_send()
    cross_p_last().wait_send()
    for copy in rows_first() + rows_last():
        copy.wait_send()
    for way in range(2):
        rs_copy(steps, way, way, last_own).wait_send()
    g_copy(steps, 0, last_own).wait_send()
    for j in range(1, ndp):
        for copy in w_copies(j):
            copy.wait_send()


def on_device(tokens, cotangent, expert_ids, gate_probs, w_gate, w_up, w_down):
    ndp, nex = lax.axis_size("dp"), lax.axis_size("expert")
    steps = nex // 4
    tok, width = tokens.shape
    ff = w_gate.shape[2]
    topk = expert_ids.shape[1]
    cut_g, cut_d = width // ndp, ff // ndp
    blocks = 4 * steps
    vmem = pl.BlockSpec(memory_space=pltpu.VMEM)
    hbm = pl.BlockSpec(memory_space=pl.ANY)
    dma = pltpu.SemaphoreType.DMA
    return pl.pallas_call(
        kernel,
        out_shape=(
            jax.ShapeDtypeStruct((tok, width), BF16),
            jax.ShapeDtypeStruct((tok, topk), BF16),
            jax.ShapeDtypeStruct((1, cut_g, ff), BF16),
            jax.ShapeDtypeStruct((1, cut_g, ff), BF16),
            jax.ShapeDtypeStruct((1, cut_d, width), BF16),
        ),
        in_specs=[vmem, vmem, hbm, hbm, hbm, hbm, hbm],
        out_specs=[vmem] * 5,
        scratch_shapes=[
            pltpu.VMEM((blocks, tok, width), BF16),
            pltpu.VMEM((blocks, tok, width), BF16),
            pltpu.VMEM((blocks, nex, tok), BF16),
            pltpu.VMEM((blocks, tok, width), BF16),
            pltpu.VMEM((blocks, nex, tok), BF16),
            pltpu.VMEM((blocks // 2, tok, width), BF16),
            pltpu.VMEM((blocks // 2, nex, tok), BF16),
            pltpu.VMEM((2, steps, tok, width), BF16),
            pltpu.VMEM((2, steps, nex, tok), BF16),
            pltpu.VMEM((width, 2 * ff), BF16),
            pltpu.VMEM((ff, width), BF16),
            pltpu.VMEM((width, 2 * ff), F32),
            pltpu.VMEM((ff, width), F32),
            pltpu.VMEM((2 * tok, 2 * ff), F32),
            pltpu.VMEM((2 * tok, ff), F32),
            pltpu.VMEM((2 * tok, 2 * ff), BF16),
            pltpu.VMEM((2 * tok, ff), BF16),
            pltpu.VMEM((ndp, cut_g, 2 * ff), BF16),
            pltpu.VMEM((ndp, cut_d, width), BF16),
            pltpu.VMEM((ndp, cut_g, 2 * ff), BF16),
            pltpu.VMEM((ndp, cut_d, width), BF16),
            dma((3, steps + 1, 2)),
            dma((3, steps + 1, 2)),
            dma((3, steps + 1, 2)),
            dma((3, steps + 1, 2)),
            dma((2, steps + 1)),
            dma((2, steps + 1)),
            dma((2, 2, steps)),
            dma((2, 2, steps)),
            dma((2, steps)),
            dma((2, steps)),
            dma((2, ndp)),
            dma((2, ndp)),
            dma((5,)),
        ],
        compiler_params=pltpu.CompilerParams(
            collective_id=0, has_side_effects=True, vmem_limit_bytes=63 * 1024 * 1024
        ),
        name="moe_backward",
    )(expert_ids, gate_probs, tokens, cotangent, w_gate, w_up, w_down)


def solution(mesh):
    return jax.shard_map(
        on_device,
        mesh=mesh,
        in_specs=(
            P(("dp", "expert"), None),
            P(("dp", "expert"), None),
            P(("dp", "expert"), None),
            P(("dp", "expert"), None),
            P("expert", None, None),
            P("expert", None, None),
            P("expert", None, None),
        ),
        out_specs=(
            P(("dp", "expert"), None),
            P(("dp", "expert"), None),
            P("expert", "dp", None),
            P("expert", "dp", None),
            P("expert", "dp", None),
        ),
        check_vma=False,
    )
```

time: 666 us -> 165 us (0.25)
  waiting for transfers between devices: 470 us -> 0 us
  Pallas kernels: 0 us -> 156 us
  local copies, waits for them, and re-layouts: 78 us -> 7.47 us
  starting transfers between devices: 46.4 us -> 0 us
  matrix products: 28.1 us -> 0 us
  other arithmetic: 28 us -> 0 us
  between operations: 14 us -> 0.65 us
    all_to_all x5 -> x0, waiting for transfers between devices: 318 us -> none  [the longest x1 114 us: on_device(): lax.all_to_all(x_slots, 'expert', split_axis=0, concat_axis=1, tiled=True)]
    pallas_call x0 -> x1, Pallas kernels: none -> 156 us  [on_device(): pl.pallas_call(kernel, out_shape=(jax.ShapeDtypeStruct((tok, width), BF16...]
    reduce_scatter x2 -> x0, waiting for transfers between devices: 153 us -> none  [the longest x1 93.2 us: on_device(): lax.psum_scatter(grad_gate_part.astype(jnp.bfloat16), 'dp', scatter_dimen...]
    all_to_all x5 -> x0, starting transfers between devices: 46 us -> none  [the longest x1 15.5 us: on_device(): lax.all_to_all(p_slots, 'expert', split_axis=0, concat_axis=1, tiled=True)]
    gather x5 -> x0, local copies, waits for them, and re-layouts: 28.2 us -> none  [the longest x1 7.27 us: on_device(): p_slots = p_flat[filled].reshape(experts, most)]
    dot_general x8 -> x0, matrix products: 28.1 us -> none  [the longest x1 5.7 us: on_device(): jnp.einsum('erd,efd->erf', dy_recv, w_down, preferred_element_type=jnp.fl...]
    convert_element_type x3 -> x0, local copies, waits for them, and re-layouts: 17.4 us -> none  [the longest x1 16.4 us: on_device(): row_grad = (jnp.einsum('erf,edf->erd', d_gate, w_gate, preferred_element_...]
    unnamed x1 -> x0, other arithmetic: 14.2 us -> none
  transfers between devices with their start and end apart: 8 -> 0, of which waited for: 6 -> 0; matrix products, arithmetic and copies ran while one was open for 15% -> 0% of each run, Pallas kernels for 0% -> 0%
where the time goes in v1:
time: 165 us; the launch traced here: 164 us
  Pallas kernels  156 us (95%)
  local copies, waits for them, and re-layouts  7.47 us (5%)
    pallas_call x1, Pallas kernels, on_device(): pl.pallas_call(kernel, out_shape=(jax.ShapeDtypeStruct((tok, width), BF16...  156 us
    unnamed x14, local copies, waits for them, and re-layouts  6.07 us

profile of v1, /device:TPU:6, one launch (start us, length us, event | category | flops | bytes accessed | tf_op | source)
XLA Modules:
  0.0 164.3 jit_solution(10114156259931965456)
XLA Ops:
  0.6 0.0 copy-start.3
  0.6 1.4 copy.13.probs_ref
  2.0 0.0 copy-done.3
  2.0 0.7 copy.12.ids_ref
  2.8 156.2 %moe_backward.1 = (bf16[128,1024]{1,0:T(8,128)(2,1)}, bf16[128,8]{1,0:T(8,128)(2,1)}, bf16[1,64,384]{2,1,0:T(8,128)(2,1)}, bf16[1,64,384]{2,1,0:T(8,128)(2,1)}, bf16[1,24,1024]{2,1,0:T(8,128)(2,1)}) custom-call(s32[128,8]{1,0:T(8,128)} %copy.12.ids_ref, bf16[128,8]{1,0:T(8,128)(2,1)} %copy.13.probs_ref, bf16[128,1024]{1,0:T(8,128)(2,1)} %x_ref.1, ...), custom_call_target="tpu_custom_call" | custom-call | tf_op jit(solution)/shard_map/moe_backward/pallas_call | solution.py:445
  159.0 1.4 copy.14
  160.4 0.0 copy-start.2
  160.4 1.7 %copy.19 = bf16[128,1024]{1,0:T(8,128)(2,1)} copy(bf16[128,1024]{1,0:T(8,128)(2,1)} %get-tuple-element.15) | data formatting | bytes 524288
  162.0 0.0 copy-done.2
  162.0 0.0 copy-start.1
  162.0 0.6 copy.20
  162.7 0.2 copy-done.1
  162.9 0.0 copy-start
  162.9 0.6 copy.21
  163.5 0.2 copy-done
  163.7 0.6 copy.22
Async XLA Ops:
  0.6 1.4 copy-start.3
  160.4 1.7 %copy-start.2 = (bf16[1,64,384]{2,1,0:T(8,128)(2,1)S(1)}, bf16[1,64,384]{2,1,0:T(8,128)(2,1)}, u32[]{:S(2)}) copy-start(bf16[1,64,384]{2,1,0:T(8,128)(2,1)} %get-tuple-element.17) | copy-start | bytes 147460
  162.0 0.8 copy-start.1
  162.9 0.8 copy-start

commit v2 on v1

--- a/solution.py
+++ b/solution.py
@@ -33,7 +33,7 @@
     half = tok // 2
     ff = wd.shape[0]
     experts = p_all.shape[1]
-    topk = ids_ref.shape[1]
+    topk = ids_ref.shape[0]
     cut_g, cut_d = width // ndp, ff // ndp
     right = (me_dp, lax.rem(me + 2, nex))
     left = (me_dp, lax.rem(me + nex - 2, nex))
@@ -71,10 +71,11 @@
         send(src, streams[k].at[1], pc_s.at[k, 0, 0], pc_r.at[k, 0, 0], partner).start()
 
     lane = lax.broadcasted_iota(jnp.int32, (tok, LANES), 1)
-    table = jnp.zeros((tok, LANES), F32)
+    line = lax.broadcasted_iota(jnp.int32, (experts, tok), 0)
+    table = jnp.zeros((experts, tok), F32)
     for k in range(topk):
-        table = jnp.where(lane == ids_ref[:, k : k + 1], probs_ref[:, k : k + 1].astype(F32), table)
-    p_all[0] = table.T[:experts].astype(BF16)
+        table = jnp.where(line == ids_ref[k : k + 1, :], probs_ref[k : k + 1, :].astype(F32), table)
+    p_all[0] = table.astype(BF16)
     acc_gu[...] = jnp.zeros_like(acc_gu)
     acc_d[...] = jnp.zeros_like(acc_d)
     for way in range(2):
@@ -215,6 +216,9 @@
         for n in range(width // STEP):
             cols = pl.ds(n * STEP, STEP)
             rows[at, :, cols] = contract(dgu[...], wgu[cols, :], 1, 1).astype(BF16).reshape(2, tok, STEP)
+
+    def gather_weights(u):
+        at = pl.ds(2 * u, 2)
         for n in range(width // STEP):
             cols = pl.ds(n * STEP, STEP)
             acc_gu[cols, :] += contract(x_all[at, :, cols].reshape(wide, STEP), dgu[...], 0, 0)
@@ -312,6 +316,7 @@
             for copy in rows_last():
                 copy.start()
 
+        gather_weights(u)
         return carry
 
     lax.fori_loop(0, 2 * steps, unit, 0)
@@ -354,6 +359,18 @@
         return carry
 
     lax.fori_loop(0, steps - 1, ring, 0)
+
+    for j in range(1, ndp):
+        for copy in w_copies(j):
+            copy.wait_recv()
+    sum_g = stage_g[me_dp].astype(F32)
+    sum_d = stage_d[me_dp].astype(F32)
+    for j in range(1, ndp):
+        sum_g = sum_g + land_g[j].astype(F32)
+        sum_d = sum_d + land_d[j].astype(F32)
+    og_ref[0] = sum_g[:, :ff].astype(BF16)
+    ou_ref[0] = sum_g[:, ff:].astype(BF16)
+    od_ref[0] = sum_d.astype(BF16)
 
     for copy in rows_first():
         copy.wait_recv()
@@ -368,27 +385,10 @@
         total = total + land[0, 0, some].astype(F32) + land[1, 0, some].astype(F32)
         gt_ref[some, :] = total.astype(BF16)
     gsum = grows[0].astype(F32) + gpart[0].astype(F32) + gland[0, 0].astype(F32) + gland[1, 0].astype(F32)
-    if experts < LANES:
-        gsum = jnp.concatenate([gsum, jnp.zeros((LANES - experts, tok), F32)], axis=0)
-    gtab = gsum.T
     picked = []
     for k in range(topk):
-        picked.append(
-            jnp.sum(jnp.where(lane == ids_ref[:, k : k + 1], gtab, 0.0), axis=1, keepdims=True)
-        )
-    gp_ref[...] = jnp.concatenate(picked, axis=1).astype(BF16)
-
-    for j in range(1, ndp):
-        for copy in w_copies(j):
-            copy.wait_recv()
-    sum_g = stage_g[me_dp].astype(F32)
-    sum_d = stage_d[me_dp].astype(F32)
-    for j in range(1, ndp):
-        sum_g = sum_g + land_g[j].astype(F32)
-        sum_d = sum_d + land_d[j].astype(F32)
-    og_ref[0] = sum_g[:, :ff].astype(BF16)
-    ou_ref[0] = sum_g[:, ff:].astype(BF16)
-    od_ref[0] = sum_d.astype(BF16)
+        picked.append(jnp.sum(jnp.where(line == ids_ref[k : k + 1, :], gsum, 0.0), axis=0, keepdims=True))
+    gp_ref[...] = jnp.concatenate(picked, axis=0).astype(BF16)
 
     for k, src in ((0, x_ref), (1, dy_ref), (2, p_all.at[0])):
         ref = (x_all, dy_all, p_all)[k]
@@ -431,6 +431,11 @@
             copy.wait_send()
 
 
+def hand_on(*refs):
+    for src, dst in zip(refs[:5], refs[5:]):
+        dst[...] = src[...]
+
+
 def on_device(tokens, cotangent, expert_ids, gate_probs, w_gate, w_up, w_down):
     ndp, nex = lax.axis_size("dp"), lax.axis_size("expert")
     steps = nex // 4
@@ -442,11 +447,11 @@
     vmem = pl.BlockSpec(memory_space=pltpu.VMEM)
     hbm = pl.BlockSpec(memory_space=pl.ANY)
     dma = pltpu.SemaphoreType.DMA
-    return pl.pallas_call(
+    outs = pl.pallas_call(
         kernel,
         out_shape=(
             jax.ShapeDtypeStruct((tok, width), BF16),
-            jax.ShapeDtypeStruct((tok, topk), BF16),
+            jax.ShapeDtypeStruct((topk, tok), BF16),
             jax.ShapeDtypeStruct((1, cut_g, ff), BF16),
             jax.ShapeDtypeStruct((1, cut_g, ff), BF16),
             jax.ShapeDtypeStruct((1, cut_d, width), BF16),
@@ -493,7 +498,15 @@
             collective_id=0, has_side_effects=True, vmem_limit_bytes=63 * 1024 * 1024
         ),
         name="moe_backward",
-    )(expert_ids, gate_probs, tokens, cotangent, w_gate, w_up, w_down)
+    )(expert_ids.T, gate_probs.T, tokens, cotangent, w_gate, w_up, w_down)
+    outs = pl.pallas_call(
+        hand_on,
+        out_shape=[jax.ShapeDtypeStruct(v.shape, v.dtype) for v in outs],
+        in_specs=[vmem] * 5,
+        out_specs=[vmem] * 5,
+        name="hand_on",
+    )(*outs)
+    return outs[0], outs[1].T, outs[2], outs[3], outs[4]
 
 
 def solution(mesh):

time: 165 us -> 158 us (0.958)
  local copies, waits for them, and re-layouts: 7.47 us -> 0 us
    unnamed x14 -> x0, local copies, waits for them, and re-layouts: 6.07 us -> none
    pallas_call x1, Pallas kernels: 156 us -> 154 us  [on_device(): pl.pallas_call(kernel, out_shape=(jax.ShapeDtypeStruct((tok, width), BF16...]
    pallas_call x0 -> x1, Pallas kernels: none -> 1.74 us  [on_device(): pl.pallas_call(hand_on, out_shape=[jax.ShapeDtypeStruct(v.shape, v.dtype)...]
where the time goes in v2:
time: 158 us; the launch traced here: 157 us
  Pallas kernels  156 us (99%)
    pallas_call x1, Pallas kernels, on_device(): pl.pallas_call(kernel, out_shape=(jax.ShapeDtypeStruct((tok, width), BF16...  154 us

profile of v2, /device:TPU:6, one launch (start us, length us, event | category | flops | bytes accessed | tf_op | source)
XLA Modules:
  0.0 156.8 jit_solution(7632259579971309232)
XLA Ops:
  0.6 154.4 %moe_backward.1 = (bf16[128,1024]{1,0:T(8,128)(2,1)}, bf16[8,128]{1,0:T(8,128)(2,1)}, bf16[1,64,384]{2,1,0:T(8,128)(2,1)}, bf16[1,64,384]{2,1,0:T(8,128)(2,1)}, bf16[1,24,1024]{2,1,0:T(8,128)(2,1)}) custom-call(s32[8,128]{1,0:T(8,128)} %bitcast.3, bf16[8,128]{1,0:T(8,128)(2,1)} %bitcast.4, bf16[128,1024]{1,0:T(8,128)(2,1)} %x_ref.1, ...), custom_call_target="tpu_custom_call" | custom-call | tf_op jit(solution)/shard_map/moe_backward/pallas_call | solution.py:450
  155.0 1.7 %hand_on.1 = (bf16[128,1024]{1,0:T(8,128)(2,1)}, bf16[8,128]{1,0:T(8,128)(2,1)}, bf16[1,64,384]{2,1,0:T(8,128)(2,1)}, bf16[1,64,384]{2,1,0:T(8,128)(2,1)}, bf16[1,24,1024]{2,1,0:T(8,128)(2,1)}) custom-call(bf16[128,1024]{1,0:T(8,128)(2,1)} %get-tuple-element.15.refs_0_, bf16[8,128]{1,0:T(8,128)(2,1)} %get-tuple-element.16.refs_1_, ...), custom_call_target="tpu_custom_call" | custom-call | tf_op jit(solution)/shard_map/hand_on/pallas_call | solution.py:502

commit v3 on v2

--- a/solution.py
+++ b/solution.py
@@ -12,6 +12,7 @@
 BF16 = jnp.bfloat16
 LANES = 128
 STEP = 256
+SIDE = 4
 
 
 def contract(a, b, on_a, on_b):
@@ -24,7 +25,7 @@
     x_all, dy_all, p_all, rows, grows, rpart, gpart, land, gland,
     wgu, wd, acc_gu, acc_d, gu, dz, dgu, hp,
     stage_g, stage_d, land_g, land_d,
-    ag_s, ag_r, pc_s, pc_r, rp_s, rp_r, rs_s, rs_r, g_s, g_r, w_s, w_r, loc,
+    ag_s, ag_r, pc_s, pc_r, rp_s, rp_r, rs_s, rs_r, g_s, g_r, w_s, w_r, loc, ready_sem,
 ):
     ndp, nex = lax.axis_size("dp"), lax.axis_size("expert")
     me_dp, me = lax.axis_index("dp"), lax.axis_index("expert")
@@ -47,8 +48,20 @@
         )
 
     barrier = pltpu.get_barrier_semaphore()
-    for dev in [right, left, partner] + peers:
+    for dev in (right, left, partner):
         pl.semaphore_signal(barrier, inc=1, device_id=dev, device_id_type=MESH)
+
+    def turn(dp):
+        return (jnp.minimum(dp // SIDE, 2) + jnp.minimum(lax.rem(dp, SIDE), 2)) * ndp + dp
+
+    ahead = [turn(dev[0]) < turn(me_dp) for dev in peers]
+    for dev, first in zip(peers, ahead):
+
+        @pl.when(jnp.logical_not(first))
+        def _():
+            pl.semaphore_signal(barrier, inc=1, device_id=dev, device_id_type=MESH)
+
+    n_ahead = sum([jnp.where(first, 1, 0) for first in ahead], jnp.int32(0))
     local = [
         pltpu.make_async_copy(x_ref, x_all.at[0], loc.at[0]),
         pltpu.make_async_copy(dy_ref, dy_all.at[0], loc.at[1]),
@@ -58,7 +71,7 @@
     ]
     for copy in local:
         copy.start()
-    pl.semaphore_wait(barrier, 3 + len(peers))
+    pl.semaphore_wait(barrier, 3 + n_ahead)
 
     streams = (x_all, dy_all)
 
@@ -69,6 +82,12 @@
         for way in range(2):
             send(src, streams[k].at[own_slot(1, way)], ag_s.at[k, 1, way], ag_r.at[k, 1, way], toward[way]).start()
         send(src, streams[k].at[1], pc_s.at[k, 0, 0], pc_r.at[k, 0, 0], partner).start()
+
+    for dev, first in zip(peers, ahead):
+
+        @pl.when(first)
+        def _():
+            pl.semaphore_signal(ready_sem, inc=1, device_id=dev, device_id_type=MESH)
 
     lane = lax.broadcasted_iota(jnp.int32, (tok, LANES), 1)
     line = lax.broadcasted_iota(jnp.int32, (experts, tok), 0)
@@ -337,6 +356,11 @@
         stage_g[n] = acc_gu[n * cut_g : (n + 1) * cut_g, :].astype(BF16)
     for n in range(ndp):
         stage_d[n] = acc_d[n * cut_d : (n + 1) * cut_d, :].astype(BF16)
+
+    @pl.when(n_ahead < len(peers))
+    def _():
+        pl.semaphore_wait(ready_sem, len(peers) - n_ahead)
+
     for j in range(1, ndp):
         for copy in w_copies(j):
             copy.start()
@@ -493,6 +517,7 @@
             dma((2, ndp)),
             dma((2, ndp)),
             dma((5,)),
+            pltpu.SemaphoreType.REGULAR,
         ],
         compiler_params=pltpu.CompilerParams(
             collective_id=0, has_side_effects=True, vmem_limit_bytes=63 * 1024 * 1024

time: 158 us -> 156 us (0.987)
  Pallas kernels: 156 us -> 154 us
    pallas_call x1, Pallas kernels: 154 us -> 152 us  [on_device(): pl.pallas_call(kernel, out_shape=(jax.ShapeDtypeStruct((tok, width), BF16...]
where the time goes in v3:
time: 156 us; the launch traced here: 155 us
  Pallas kernels  154 us (99%)
    pallas_call x1, Pallas kernels, on_device(): pl.pallas_call(kernel, out_shape=(jax.ShapeDtypeStruct((tok, width), BF16...  152 us

profile of v3, /device:TPU:6, one launch (start us, length us, event | category | flops | bytes accessed | tf_op | source)
XLA Modules:
  0.0 154.8 jit_solution(17893526280538381872)
XLA Ops:
  0.6 152.4 %moe_backward.1 = (bf16[128,1024]{1,0:T(8,128)(2,1)}, bf16[8,128]{1,0:T(8,128)(2,1)}, bf16[1,64,384]{2,1,0:T(8,128)(2,1)}, bf16[1,64,384]{2,1,0:T(8,128)(2,1)}, bf16[1,24,1024]{2,1,0:T(8,128)(2,1)}) custom-call(s32[8,128]{1,0:T(8,128)} %bitcast.3, bf16[8,128]{1,0:T(8,128)(2,1)} %bitcast.4, bf16[128,1024]{1,0:T(8,128)(2,1)} %x_ref.1, ...), custom_call_target="tpu_custom_call" | custom-call | tf_op jit(solution)/shard_map/moe_backward/pallas_call | solution.py:474
  153.1 1.7 %hand_on.1 = (bf16[128,1024]{1,0:T(8,128)(2,1)}, bf16[8,128]{1,0:T(8,128)(2,1)}, bf16[1,64,384]{2,1,0:T(8,128)(2,1)}, bf16[1,64,384]{2,1,0:T(8,128)(2,1)}, bf16[1,24,1024]{2,1,0:T(8,128)(2,1)}) custom-call(bf16[128,1024]{1,0:T(8,128)(2,1)} %get-tuple-element.15.refs_0_, bf16[8,128]{1,0:T(8,128)(2,1)} %get-tuple-element.16.refs_1_, ...), custom_call_target="tpu_custom_call" | custom-call | tf_op jit(solution)/shard_map/hand_on/pallas_call | solution.py:527
